TPU v7x, 256 devices: a whole 4x4x8 slice. The times are simulated.
256 devices in a mesh: seq: 16 (over x, z_hi), wt: 16 (over z_lo, y, core).
Axes of the slice: x: 4, y: 4, z: 8 (z_hi: 4, z_lo: 2; z = z_hi * 2 + z_lo), core: 2. Of those that a mesh axis runs over, the one named last changes fastest.
Arguments:
- queries: bfloat16 [4096, 5120], P('seq', 'wt'), may hold values from -6 to 6
- keys: bfloat16 [4096, 5120], P('seq', 'wt'), may hold values from -6 to 6
- values: bfloat16 [4096, 5120], P('seq', 'wt'), may hold values from -6 to 6
- rates: float32 [4096], P('seq'), may hold values from 0.2 to 1.5
- w_gate: bfloat16 [5120, 5120], P('seq', 'wt'), may hold values from -0.078125 to 0.078125
- w_up: bfloat16 [5120, 5120], P('seq', 'wt'), may hold values from -0.078125 to 0.078125
- w_down: bfloat16 [5120, 5120], P('seq', 'wt'), may hold values from -0.078125 to 0.078125
Outputs:
- mixed: bfloat16 [4096, 5120], P('seq', 'wt')
- new_gate: bfloat16 [5120, 5120], P('seq', 'wt')
- new_up: bfloat16 [5120, 5120], P('seq', 'wt')
- new_down: bfloat16 [5120, 5120], P('seq', 'wt')
All inputs are finite; a program needn't handle non-finite values.
Results may differ from a plain program's by a relative error of at most 0.03.
Values may be sent and summed in bfloat16 or wider, within the bound.
No kernel may reach another device: no remote copies, remote signals or barrier semaphores. Data moves between devices by JAX's collectives and lax.ppermute only.
A program may use at most 64 MiB of HBM per device.

v0:
```python
import jax
import jax.numpy as jnp
from jax import lax
from jax.sharding import PartitionSpec as P


def contract_rows(matrix_left, matrix_right):
    return lax.dot_general(
        matrix_left, matrix_right, (((0,), (0,)), ((), ())), preferred_element_type=jnp.float32
    )


def local(queries, keys, values, rates, w_gate, w_up, w_down):
    queries_all, keys_all, values_all = (
        lax.all_gather(queries, "wt", axis=1, tiled=True),
        lax.all_gather(keys, "wt", axis=1, tiled=True),
        lax.all_gather(values, "wt", axis=1, tiled=True),
    )
    row_count = keys.shape[0]
    hidden_local = w_gate.shape[1]
    token_count = row_count * lax.axis_size("seq")
    hidden_count = hidden_local * lax.axis_size("wt")
    token_rate = rates * lax.rsqrt(jnp.float32(token_count * hidden_count))
    scaled_values = (token_rate[:, None] * values_all.astype(jnp.float32)).astype(jnp.bfloat16)
    pieces = (
        lax.all_gather(w_gate, "seq", axis=0, tiled=True),
        lax.all_gather(w_up, "seq", axis=0, tiled=True),
        lax.all_gather(w_down, "seq", axis=0, tiled=True),
    )
    key_cols = keys_all
    value_cols = scaled_values
    gate_pre = jnp.dot(key_cols, pieces[0], preferred_element_type=jnp.float32)
    up_pre = jnp.dot(key_cols, pieces[1], preferred_element_type=jnp.float32)
    hidden_grad = jnp.dot(value_cols, pieces[2], preferred_element_type=jnp.float32)
    sigmoid_gate = jax.nn.sigmoid(gate_pre)
    silu_gate = gate_pre * sigmoid_gate
    hidden_keys = (silu_gate * up_pre).astype(jnp.bfloat16)
    gate_grad = (
        hidden_grad * up_pre * sigmoid_gate * (1.0 + gate_pre * (1.0 - sigmoid_gate))
    ).astype(jnp.bfloat16)
    up_grad = (hidden_grad * silu_gate).astype(jnp.bfloat16)
    key_cols = keys_all
    value_cols = scaled_values
    grads = lax.psum_scatter(
        jnp.concatenate(
            [
                contract_rows(key_cols, gate_grad),
                contract_rows(key_cols, up_grad),
                contract_rows(value_cols, hidden_keys),
            ],
            axis=1,
        ).astype(jnp.bfloat16),
        "seq",
        scatter_dimension=0,
        tiled=True,
    ).astype(jnp.float32)
    new_gate = (w_gate.astype(jnp.float32) + grads[:, :hidden_local]).astype(jnp.bfloat16)
    new_up = (w_up.astype(jnp.float32) + grads[:, hidden_local : 2 * hidden_local]).astype(
        jnp.bfloat16
    )
    new_down = (w_down.astype(jnp.float32) + grads[:, 2 * hidden_local :]).astype(jnp.bfloat16)
    pieces = (
        lax.all_gather(new_gate, "seq", axis=0, tiled=True),
        lax.all_gather(new_up, "seq", axis=0, tiled=True),
    )
    gate_query = jnp.dot(queries_all, pieces[0], preferred_element_type=jnp.float32)
    up_query = jnp.dot(queries_all, pieces[1], preferred_element_type=jnp.float32)
    hidden_query = (jax.nn.silu(gate_query) * up_query).astype(jnp.bfloat16)
    partial_out = lax.dot_general(
        hidden_query,
        lax.all_gather(new_down, "seq", axis=0, tiled=True),
        (((1,), (1,)), ((), ())),
        preferred_element_type=jnp.float32,
    )
    mixed = lax.psum_scatter(
        partial_out.astype(jnp.bfloat16), "wt", scatter_dimension=1, tiled=True
    )
    return (mixed, new_gate, new_up, new_down)


def solution(mesh):
    return jax.shard_map(
        local,
        mesh=mesh,
        in_specs=(
            P("seq", "wt"),
            P("seq", "wt"),
            P("seq", "wt"),
            P("seq"),
            P("seq", "wt"),
            P("seq", "wt"),
            P("seq", "wt"),
        ),
        out_specs=(P("seq", "wt"), P("seq", "wt"), P("seq", "wt"), P("seq", "wt")),
        check_vma=False,
    )
```

profile of v0, /device:TPU:2, one launch (start us, length us, event | category | flops | bytes accessed | tf_op | source)
XLA Modules:
  0.0 829.8 jit_solution(17764385886914328162)
XLA Ops:
  7.2 0.7 all-gather.14.cloned.1.call-update
  7.9 0.7 all-gather.18.cloned.1.call-update
  8.7 0.7 all-gather.16.cloned.1.call-update
  10.0 0.5 all-gather.12.cloned.1.call-update
  10.6 0.7 broadcast_multiply_fusion
  11.3 38.7 %all-gather.14.cloned.1.call-done = bf16[256,5120]{0,1:T(8,128)(2,1)} async-done(((bf16[256,320]{0,1:T(8,128)(2,1)}), bf16[256,5120]{0,1:T(8,128)(2,1)}) %all-gather.14.cloned.1.call-update) | async-done | bytes 2621456 | tf_op jit(solution)/shard_map/all_gather | solution.py:16
  50.0 77.5 %all-gather.18.cloned.1.call-done = bf16[5120,320]{1,0:T(8,128)(2,1)} async-done(((bf16[320,320]{1,0:T(8,128)(2,1)}), bf16[5120,320]{1,0:T(8,128)(2,1)}) %all-gather.18.cloned.1.call-update) | async-done | bytes 3276816 | tf_op jit(solution)/shard_map/all_gather | solution.py:26
  127.5 4.5 fusion.23
  132.0 71.1 %all-gather.16.cloned.1.call-done = bf16[5120,320]{1,0:T(8,128)(2,1)} async-done(((bf16[320,320]{1,0:T(8,128)(2,1)}), bf16[5120,320]{1,0:T(8,128)(2,1)}) %all-gather.16.cloned.1.call-update) | async-done | bytes 3276816 | tf_op jit(solution)/shard_map/all_gather | solution.py:27
  203.1 3.7 fusion.22
  206.8 33.2 %all-gather.10.cloned.1.call-done = bf16[256,5120]{0,1:T(8,128)(2,1)} async-done(((bf16[256,320]{0,1:T(8,128)(2,1)}), bf16[256,5120]{0,1:T(8,128)(2,1)}) %all-gather.10.cloned.1.call-update) | async-done | bytes 2621456 | tf_op jit(solution)/shard_map/all_gather | solution.py:17
  240.0 77.4 %all-gather.12.cloned.1.call-done = bf16[5120,320]{1,0:T(8,128)(2,1)} async-done(((bf16[320,320]{1,0:T(8,128)(2,1)}), bf16[5120,320]{1,0:T(8,128)(2,1)}) %all-gather.12.cloned.1.call-update) | async-done | bytes 3276816 | tf_op jit(solution)/shard_map/all_gather | solution.py:28
  317.3 4.5 fusion.2
  321.8 1.1 fusion.1
  322.9 1.1 fusion
  324.0 0.6 copy-done.5
  324.6 1.1 convolution_convert_fusion
  325.7 4.5 pad_maximum_fusion
  330.3 14.3 %copy.26 = bf16[5120,960]{1,0:T(8,128)(2,1)} copy(bf16[5120,960]{0,1:T(8,128)(2,1)} %pad_maximum_fusion) | data formatting | bytes 19660800
  344.6 0.7 all-gather.22.cloned.1.call-update
  346.1 134.6 %reduce-scatter.7.cloned.1.call-done = bf16[320,960]{1,0:T(8,128)(2,1)} async-done(((bf16[5120,960]{1,0:T(8,128)(2,1)}), bf16[320,960]{1,0:T(8,128)(2,1)}) %reduce-scatter.7.cloned.1.call-update) | async-done | bytes 614416
  480.7 1.5 copy.27
  482.5 0.9 copy.18
  483.4 0.9 copy.20
  484.3 0.9 copy.22
  485.4 33.0 %all-gather.22.cloned.1.call-done = bf16[256,5120]{0,1:T(8,128)(2,1)} async-done(((bf16[256,320]{0,1:T(8,128)(2,1)}), bf16[256,5120]{0,1:T(8,128)(2,1)}) %all-gather.22.cloned.1.call-update) | async-done | bytes 2621456 | tf_op jit(solution)/shard_map/all_gather | solution.py:15
  518.4 78.1 %all-gather.20.cloned.1.call-done = bf16[5120,320]{1,0:T(8,128)(2,1)} async-done(((bf16[320,320]{1,0:T(8,128)(2,1)}), bf16[5120,320]{1,0:T(8,128)(2,1)}) %all-gather.20.cloned.1.call-update) | async-done | bytes 3276816 | tf_op jit(solution)/shard_map/all_gather | solution.py:63
  596.5 4.2 convolution_bitcast_fusion.1
  600.7 72.0 %all-gather.24.cloned.1.call-done = bf16[5120,320]{1,0:T(8,128)(2,1)} async-done(((bf16[320,320]{1,0:T(8,128)(2,1)}), bf16[5120,320]{1,0:T(8,128)(2,1)}) %all-gather.24.cloned.1.call-update) | async-done | bytes 3276816 | tf_op jit(solution)/shard_map/all_gather | solution.py:64
  672.6 76.0 %all-gather.26.cloned.1.call-done = bf16[5120,320]{1,0:T(8,128)(2,1)} async-done(((bf16[320,320]{1,0:T(8,128)(2,1)}), bf16[5120,320]{1,0:T(8,128)(2,1)}) %all-gather.26.cloned.1.call-update) | async-done | bytes 3276816 | tf_op jit(solution)/shard_map/all_gather | solution.py:71
  748.6 9.1 %convolution_convert_fusion.3 = bf16[256,5120]{0,1:T(8,128)(2,1)} fusion(bf16[5120,320]{1,0:T(8,128)(2,1)} %all-gather.26.cloned.1.call-done, bf16[5120,320]{1,0:T(8,128)(2,1)} %all-gather.24.cloned.1.call-done, bf16[256,5120]{0,1:T(8,128)(2,1)S(1)} %copy-done.4, f32[256,320]{0,1:T(8,128)S(1)} %convolution_bitcast_fusion.1), kind=kOutput, calls=%fused_computation.4 | convolution fusion | flops 1679523840 | bytes 12124160 | tf_op jit(solution)/shard_map/dot_general | solution.py:69
  757.7 65.6 %reduce-scatter.5.cloned.1.call-done = bf16[256,320]{0,1:T(8,128)(2,1)} async-done(((bf16[256,5120]{0,1:T(8,128)(2,1)}), bf16[256,320]{0,1:T(8,128)(2,1)}) %reduce-scatter.5.cloned.1.call-update) | async-done | bytes 163856 | tf_op jit(solution)/shard_map/reduce_scatter | solution.py:75
  (33 shorter events, 2.2 us)
Async XLA Ops:
  7.2 42.8 %all-gather.14.cloned.1.call-start = ((), (), s32[]{:S(2)}) async-start(), calls=%async_computation.4 | async-start | bytes 2785280 | tf_op jit(solution)/shard_map/all_gather | solution.py:16
  7.9 119.6 %all-gather.18.cloned.1.call-start = ((), (), s32[]{:S(2)}) async-start(), calls=%async_computation.6 | async-start | bytes 4177920 | tf_op jit(solution)/shard_map/all_gather | solution.py:26
  8.6 194.4 %all-gather.16.cloned.1.call-start = ((), (), s32[]{:S(2)}) async-start(), calls=%async_computation.5 | async-start | bytes 4177920 | tf_op jit(solution)/shard_map/all_gather | solution.py:27
  9.4 230.6 %all-gather.10.cloned.1.call-start = ((), (), s32[]{:S(2)}) async-start(), calls=%async_computation.2 | async-start | bytes 2785280 | tf_op jit(solution)/shard_map/all_gather | solution.py:17
  10.0 307.4 %all-gather.12.cloned.1.call-start = ((), (), s32[]{:S(2)}) async-start(), calls=%async_computation.3 | async-start | bytes 4177920 | tf_op jit(solution)/shard_map/all_gather | solution.py:28
  10.5 470.1 %reduce-scatter.7.cloned.1.call-start = ((), (), s32[]{:S(2)}) async-start(), calls=%async_computation.12 | async-start | bytes 11141120
  50.0 153.1 %copy-start = (bf16[256,5120]{0,1:T(8,128)(2,1)S(1)}, bf16[256,5120]{0,1:T(8,128)(2,1)}, u32[]{:S(2)}) copy-start(bf16[256,5120]{0,1:T(8,128)(2,1)} %all-gather.14.cloned.1.call-done) | copy-start | bytes 7864324
  322.9 1.7 copy-start.5
  344.6 0.9 copy-start.1
  344.6 1.1 copy-start.2
  344.6 1.3 copy-start.3
  344.6 173.8 %all-gather.22.cloned.1.call-start = ((), (), s32[]{:S(2)}) async-start(), calls=%async_computation.8 | async-start | bytes 2785280 | tf_op jit(solution)/shard_map/all_gather | solution.py:15
  345.3 251.1 %all-gather.20.cloned.1.call-start = ((), (), s32[]{:S(2)}) async-start(), calls=%async_computation.7 | async-start | bytes 4177920 | tf_op jit(solution)/shard_map/all_gather | solution.py:63
  483.3 189.3 %all-gather.24.cloned.1.call-start = ((), (), s32[]{:S(2)}) async-start(), calls=%async_computation.9 | async-start | bytes 4177920 | tf_op jit(solution)/shard_map/all_gather | solution.py:64
  484.3 264.4 %all-gather.26.cloned.1.call-start = ((), (), s32[]{:S(2)}) async-start(), calls=%async_computation.10 | async-start | bytes 4177920 | tf_op jit(solution)/shard_map/all_gather | solution.py:71
  485.2 338.1 %reduce-scatter.5.cloned.1.call-start = ((), (), s32[]{:S(2)}) async-start(), calls=%async_computation.11 | async-start | bytes 2785280 | tf_op jit(solution)/shard_map/reduce_scatter | solution.py:75
  518.4 230.2 %copy-start.4 = (bf16[256,5120]{0,1:T(8,128)(2,1)S(1)}, bf16[256,5120]{0,1:T(8,128)(2,1)}, u32[]{:S(2)}) copy-start(bf16[256,5120]{0,1:T(8,128)(2,1)} %all-gather.22.cloned.1.call-done) | copy-start | bytes 7864324
Sparse Core Ops, SparseCore 0:
  9.8 40.1 all-gather.13
  52.4 74.9 all-gather.17
  130.0 73.0 all-gather.15
  204.8 35.1 all-gather.9
  242.3 74.9 all-gather.11
  344.7 135.9 reduce-scatter.6
  482.5 35.8 all-gather.21
  521.5 74.9 all-gather.19
  599.6 73.0 all-gather.23
  675.5 73.0 all-gather.25
  757.8 65.4 reduce-scatter.4
where the time goes:
time: 830 us
  waiting for transfers between devices  761 us (92%)
  matrix products  29.1 us (4%)
  local copies, waits for them, and re-layouts  19.7 us (2%)
  between operations  14 us (2%)
    unnamed x12, waiting for transfers between devices  138 us
    all_gather x1, waiting for transfers between devices, local(): lax.all_gather(new_gate, 'seq', axis=0, tiled=True)  78.1 us
    all_gather x1, waiting for transfers between devices, local(): lax.all_gather(w_gate, 'seq', axis=0, tiled=True)  77.5 us
    all_gather x1, waiting for transfers between devices, local(): lax.all_gather(w_down, 'seq', axis=0, tiled=True)  77.4 us
    all_gather x1, waiting for transfers between devices, local(): lax.all_gather(new_down, 'seq', axis=0, tiled=True)  76 us
    all_gather x1, waiting for transfers between devices, local(): lax.all_gather(new_up, 'seq', axis=0, tiled=True)  72 us
    all_gather x1, waiting for transfers between devices, local(): lax.all_gather(w_up, 'seq', axis=0, tiled=True)  71.1 us
    reduce_scatter x1, waiting for transfers between devices, local(): lax.psum_scatter(partial_out.astype(jnp.bfloat16), 'wt', scatter_dimensio...  65.6 us
  transfers between devices with their start and end apart: 11, of which 11 were waited for; matrix products, arithmetic and copies ran while one was open for 2% of the time, Pallas kernels for 0%

commit v1 on v0

--- a/solution.py
+++ b/solution.py
@@ -2,6 +2,13 @@
 import jax.numpy as jnp
 from jax import lax
 from jax.sharding import PartitionSpec as P
+
+
+def all_by_exchange(x, axis, dim):
+    size = lax.axis_size(axis)
+    pieces = jnp.stack([x for _ in range(size)])
+    pieces = lax.all_to_all(pieces, axis, split_axis=0, concat_axis=0)
+    return jnp.concatenate(pieces, axis=dim)
 
 
 def contract_rows(matrix_left, matrix_right):
@@ -68,7 +75,7 @@
     hidden_query = (jax.nn.silu(gate_query) * up_query).astype(jnp.bfloat16)
     partial_out = lax.dot_general(
         hidden_query,
-        lax.all_gather(new_down, "seq", axis=0, tiled=True),
+        all_by_exchange(new_down, "seq", 0),
         (((1,), (1,)), ((), ())),
         preferred_element_type=jnp.float32,
     )

time: 830 us -> 809 us (0.975)
  waiting for transfers between devices: 761 us -> 730 us
    all_gather x1 -> x0, waiting for transfers between devices: 76 us -> none  [local(): lax.all_gather(new_down, 'seq', axis=0, tiled=True)]
    all_gather x1, waiting for transfers between devices: 33 us -> 60.4 us  [local(): lax.all_gather(queries, 'wt', axis=1, tiled=True)]
    all_gather x1, waiting for transfers between devices: 78.1 us -> 95.7 us  [local(): lax.all_gather(new_gate, 'seq', axis=0, tiled=True)]
    unnamed x12 -> x11, waiting for transfers between devices: 138 us -> 138 us
    unnamed x17 -> x19, local copies, waits for them, and re-layouts: 17.1 us -> 17.1 us
  transfers between devices with their start and end apart: 11 -> 11, of which waited for: 11 -> 10; matrix products, arithmetic and copies ran while one was open for 2% -> 2% of each run, Pallas kernels for 0% -> 0%
where the time goes in v1:
time: 809 us; the launch traced here: 808 us
  waiting for transfers between devices  730 us (90%)
  matrix products  29.1 us (4%)
  local copies, waits for them, and re-layouts  21.4 us (3%)
  between operations  14.3 us (2%)
    unnamed x11, waiting for transfers between devices  138 us
    all_gather x1, waiting for transfers between devices, local(): lax.all_gather(new_gate, 'seq', axis=0, tiled=True)  95.7 us
    all_gather x1, waiting for transfers between devices, local(): lax.all_gather(w_gate, 'seq', axis=0, tiled=True)  77.5 us
    all_gather x1, waiting for transfers between devices, local(): lax.all_gather(w_down, 'seq', axis=0, tiled=True)  77.4 us
    all_gather x1, waiting for transfers between devices, local(): lax.all_gather(new_up, 'seq', axis=0, tiled=True)  72 us
    all_gather x1, waiting for transfers between devices, local(): lax.all_gather(w_up, 'seq', axis=0, tiled=True)  71.1 us
    reduce_scatter x1, waiting for transfers between devices, local(): lax.psum_scatter(partial_out.astype(jnp.bfloat16), 'wt', scatter_dimensio...  65.6 us
    all_gather x1, waiting for transfers between devices, local(): lax.all_gather(queries, 'wt', axis=1, tiled=True)  60.4 us
  transfers between devices with their start and end apart: 11, of which 10 were waited for; matrix products, arithmetic and copies ran while one was open for 2% of the time, Pallas kernels for 0%

profile of v1, /device:TPU:2, one launch (start us, length us, event | category | flops | bytes accessed | tf_op | source)
XLA Modules:
  0.0 808.2 jit_solution(14329430505999205754)
XLA Ops:
  7.2 0.7 all-gather.13.cloned.1.call-update
  7.9 0.7 all-gather.17.cloned.1.call-update
  8.7 0.7 all-gather.15.cloned.1.call-update
  10.0 0.5 all-gather.11.cloned.1.call-update
  10.6 0.7 broadcast_multiply_fusion
  11.3 38.7 %all-gather.13.cloned.1.call-done = bf16[256,5120]{0,1:T(8,128)(2,1)} async-done(((bf16[256,320]{0,1:T(8,128)(2,1)}), bf16[256,5120]{0,1:T(8,128)(2,1)}) %all-gather.13.cloned.1.call-update) | async-done | bytes 2621456 | tf_op jit(solution)/shard_map/all_gather | solution.py:23
  50.0 77.5 %all-gather.17.cloned.1.call-done = bf16[5120,320]{1,0:T(8,128)(2,1)} async-done(((bf16[320,320]{1,0:T(8,128)(2,1)}), bf16[5120,320]{1,0:T(8,128)(2,1)}) %all-gather.17.cloned.1.call-update) | async-done | bytes 3276816 | tf_op jit(solution)/shard_map/all_gather | solution.py:33
  127.5 4.5 fusion.23
  132.0 71.1 %all-gather.15.cloned.1.call-done = bf16[5120,320]{1,0:T(8,128)(2,1)} async-done(((bf16[320,320]{1,0:T(8,128)(2,1)}), bf16[5120,320]{1,0:T(8,128)(2,1)}) %all-gather.15.cloned.1.call-update) | async-done | bytes 3276816 | tf_op jit(solution)/shard_map/all_gather | solution.py:34
  203.1 3.7 fusion.22
  206.8 33.2 %all-gather.9.cloned.1.call-done = bf16[256,5120]{0,1:T(8,128)(2,1)} async-done(((bf16[256,320]{0,1:T(8,128)(2,1)}), bf16[256,5120]{0,1:T(8,128)(2,1)}) %all-gather.9.cloned.1.call-update) | async-done | bytes 2621456 | tf_op jit(solution)/shard_map/all_gather | solution.py:24
  240.0 77.4 %all-gather.11.cloned.1.call-done = bf16[5120,320]{1,0:T(8,128)(2,1)} async-done(((bf16[320,320]{1,0:T(8,128)(2,1)}), bf16[5120,320]{1,0:T(8,128)(2,1)}) %all-gather.11.cloned.1.call-update) | async-done | bytes 3276816 | tf_op jit(solution)/shard_map/all_gather | solution.py:35
  317.3 4.5 fusion.2
  321.8 1.1 fusion.1
  322.9 1.1 fusion
  324.0 0.6 copy-done.6
  324.6 1.1 convolution_convert_fusion
  325.7 4.5 pad_maximum_fusion
  330.3 14.3 %copy.27 = bf16[5120,960]{1,0:T(8,128)(2,1)} copy(bf16[5120,960]{0,1:T(8,128)(2,1)} %pad_maximum_fusion) | data formatting | bytes 19660800
  344.6 0.7 all-gather.21.cloned.1.call-update
  346.1 134.6 %reduce-scatter.7.cloned.1.call-done = bf16[320,960]{1,0:T(8,128)(2,1)} async-done(((bf16[5120,960]{1,0:T(8,128)(2,1)}), bf16[320,960]{1,0:T(8,128)(2,1)}) %reduce-scatter.7.cloned.1.call-update) | async-done | bytes 614416
  480.7 1.5 copy.28
  482.5 0.9 copy.19
  483.5 2.4 stack.2
  485.9 7.3 all-to-all-start
  493.3 0.9 copy.21
  494.4 60.4 %all-gather.21.cloned.1.call-done = bf16[256,5120]{0,1:T(8,128)(2,1)} async-done(((bf16[256,320]{0,1:T(8,128)(2,1)}), bf16[256,5120]{0,1:T(8,128)(2,1)}) %all-gather.21.cloned.1.call-update) | async-done | bytes 2621456 | tf_op jit(solution)/shard_map/all_gather | solution.py:22
  554.8 95.7 %all-gather.19.cloned.1.call-done = bf16[5120,320]{1,0:T(8,128)(2,1)} async-done(((bf16[320,320]{1,0:T(8,128)(2,1)}), bf16[5120,320]{1,0:T(8,128)(2,1)}) %all-gather.19.cloned.1.call-update) | async-done | bytes 3276816 | tf_op jit(solution)/shard_map/all_gather | solution.py:70
  650.5 4.2 convolution_bitcast_fusion.1
  654.7 72.0 %all-gather.23.cloned.1.call-done = bf16[5120,320]{1,0:T(8,128)(2,1)} async-done(((bf16[320,320]{1,0:T(8,128)(2,1)}), bf16[5120,320]{1,0:T(8,128)(2,1)}) %all-gather.23.cloned.1.call-update) | async-done | bytes 3276816 | tf_op jit(solution)/shard_map/all_gather | solution.py:71
  726.6 9.1 %convolution_convert_fusion.3 = bf16[256,5120]{0,1:T(8,128)(2,1)} fusion(bf16[5120,320]{1,0:T(8,128)(2,1)} %bitcast.4, bf16[5120,320]{1,0:T(8,128)(2,1)} %all-gather.23.cloned.1.call-done, bf16[256,5120]{0,1:T(8,128)(2,1)S(1)} %copy-done.5, f32[256,320]{0,1:T(8,128)S(1)} %convolution_bitcast_fusion.1), kind=kOutput, calls=%fused_computation.4 | convolution fusion | flops 1679523840 | bytes 12124160 | tf_op jit(solution)/shard_map/dot_general | solution.py:76
  735.7 65.6 %reduce-scatter.5.cloned.1.call-done = bf16[256,320]{0,1:T(8,128)(2,1)} async-done(((bf16[256,5120]{0,1:T(8,128)(2,1)}), bf16[256,320]{0,1:T(8,128)(2,1)}) %reduce-scatter.5.cloned.1.call-update) | async-done | bytes 163856 | tf_op jit(solution)/shard_map/reduce_scatter | solution.py:82
  (35 shorter events, 2.4 us)
Async XLA Ops:
  7.2 42.8 %all-gather.13.cloned.1.call-start = ((), (), s32[]{:S(2)}) async-start(), calls=%async_computation.5 | async-start | bytes 2785280 | tf_op jit(solution)/shard_map/all_gather | solution.py:23
  7.9 119.6 %all-gather.17.cloned.1.call-start = ((), (), s32[]{:S(2)}) async-start(), calls=%async_computation.7 | async-start | bytes 4177920 | tf_op jit(solution)/shard_map/all_gather | solution.py:33
  8.6 194.4 %all-gather.15.cloned.1.call-start = ((), (), s32[]{:S(2)}) async-start(), calls=%async_computation.6 | async-start | bytes 4177920 | tf_op jit(solution)/shard_map/all_gather | solution.py:34
  9.4 230.6 %all-gather.9.cloned.1.call-start = ((), (), s32[]{:S(2)}) async-start(), calls=%async_computation.3 | async-start | bytes 2785280 | tf_op jit(solution)/shard_map/all_gather | solution.py:24
  10.0 307.4 %all-gather.11.cloned.1.call-start = ((), (), s32[]{:S(2)}) async-start(), calls=%async_computation.4 | async-start | bytes 4177920 | tf_op jit(solution)/shard_map/all_gather | solution.py:35
  10.5 470.1 %reduce-scatter.7.cloned.1.call-start = ((), (), s32[]{:S(2)}) async-start(), calls=%async_computation.12 | async-start | bytes 11141120
  50.0 153.1 %copy-start = (bf16[256,5120]{0,1:T(8,128)(2,1)S(1)}, bf16[256,5120]{0,1:T(8,128)(2,1)}, u32[]{:S(2)}) copy-start(bf16[256,5120]{0,1:T(8,128)(2,1)} %all-gather.13.cloned.1.call-done) | copy-start | bytes 7864324
  322.9 1.7 copy-start.6
  344.6 0.9 copy-start.1
  344.6 1.1 copy-start.2
  344.6 1.3 copy-start.3
  344.6 210.2 %all-gather.21.cloned.1.call-start = ((), (), s32[]{:S(2)}) async-start(), calls=%async_computation.9 | async-start | bytes 2785280 | tf_op jit(solution)/shard_map/all_gather | solution.py:22
  345.3 305.1 %all-gather.19.cloned.1.call-start = ((), (), s32[]{:S(2)}) async-start(), calls=%async_computation.8 | async-start | bytes 4177920 | tf_op jit(solution)/shard_map/all_gather | solution.py:70
  483.5 2.4 copy-start.4
  485.9 168.7 %all-to-all-start = ((bf16[16,320,320]{2,1,0:T(8,128)(2,1)}), bf16[16,320,320]{2,1,0:T(8,128)(2,1)}, u32[]{:S(2)}, u32[]{:S(2)}) async-start(bf16[16,320,320]{2,1,0:T(8,128)(2,1)} %stack.2), calls=%async_computation | async-start | bytes 7864320 | tf_op jit(solution)/shard_map/all_to_all | solution.py:10
  493.2 233.4 %all-gather.23.cloned.1.call-start = ((), (), s32[]{:S(2)}) async-start(), calls=%async_computation.10 | async-start | bytes 4177920 | tf_op jit(solution)/shard_map/all_gather | solution.py:71
  494.2 307.2 %reduce-scatter.5.cloned.1.call-start = ((), (), s32[]{:S(2)}) async-start(), calls=%async_computation.11 | async-start | bytes 2785280 | tf_op jit(solution)/shard_map/reduce_scatter | solution.py:82
  554.8 171.8 %copy-start.5 = (bf16[256,5120]{0,1:T(8,128)(2,1)S(1)}, bf16[256,5120]{0,1:T(8,128)(2,1)}, u32[]{:S(2)}) copy-start(bf16[256,5120]{0,1:T(8,128)(2,1)} %all-gather.21.cloned.1.call-done) | copy-start | bytes 7864324
Sparse Core Ops, SparseCore 0:
  9.8 40.1 all-gather.12
  52.4 74.9 all-gather.16
  130.0 73.0 all-gather.14
  204.8 35.1 all-gather.8
  242.3 74.9 all-gather.10
  344.7 135.9 reduce-scatter.6
  482.5 72.2 all-gather.20
  557.9 92.5 all-gather.18
  653.5 73.0 all-gather.22
  735.8 65.4 reduce-scatter.4
